TPU v7x, 256 devices: a whole 4x4x8 slice. The times are simulated.
256 devices in a mesh: gen: 32 (over z, y_lo, core), neur: 4 (over x), box: 2 (over y_hi).
Axes of the slice: x: 4, y: 4 (y_hi: 2, y_lo: 2; y = y_hi * 2 + y_lo), z: 8, core: 2. Of those that a mesh axis runs over, the one named last changes fastest.
Arguments:
- gens: bfloat16 [8, 1024, 4096], P('box', 'gen'), may hold values from -1 to 1
- center: bfloat16 [8, 4096], P('box'), may hold values from -6 to 6
- weight: bfloat16 [4096, 2048], P('gen', 'neur'), may hold values from -0.09375 to 0.09375
- bias: float32 [2048], P('neur'), may hold values from -3 to 3
- phase: int32 [8, 2048], P('box', 'neur'), may hold values from 0 to 2
- gens_cot: bfloat16 [8, 1024, 2048], P('box', 'gen', 'neur'), may hold values from -6 to 6
- center_cot: float32 [8, 2048], P('box', 'neur'), may hold values from -6 to 6
- offset_cot: float32 [8, 2048], P('box', 'neur'), may hold values from -6 to 6
Outputs:
- center_out: float32 [8, 2048], P('box', 'neur')
- gens_out: bfloat16 [8, 1024, 2048], P('box', 'gen', 'neur')
- offset: float32 [8, 2048], P('box', 'neur')
- weight_grad: float32 [4096, 2048], P('gen', 'neur')
- bias_grad: float32 [2048], P('neur')
- gens_grad: float32 [8, 1024, 4096], P('box', 'gen', 'neur')
- center_grad: float32 [8, 4096], P('box', 'neur')
Inputs may be any that keep to these rules, and one draw needn't show every extreme that they name: `phase`: 0 marks an inactive neuron, 1 an active one, 2 one that crosses zero.
All inputs are finite; a program needn't handle non-finite values.
Results may differ from a plain program's by a relative error of at most 0.006.
Values may be sent and summed in bfloat16 or wider, within the bound.
A program may use at most 64 MiB of HBM per device.

v0:
```python
import jax
import jax.numpy as jnp
from jax import lax
from jax.sharding import PartitionSpec as P


def neuron(center_pre, radius, phase):
    upper = center_pre + radius
    lower = center_pre - radius
    ratio = jnp.clip(upper / (upper - lower + 1e-05), 0.0, 1.0)
    active = (phase == 1).astype(center_pre.dtype)
    crossing = (phase == 2).astype(center_pre.dtype)
    slope = active + crossing * ratio
    offset = crossing * (-ratio * lower * 0.5)
    return (slope, slope * center_pre + offset, offset)


def body(gens, center, weight, bias, phase, gens_cot, center_cot, offset_cot):
    box_dev, gen_dev, width = gens.shape
    local_cols = weight.shape[1]
    local_rows = box_dev * gen_dev
    wide = jnp.concatenate([gens.reshape(local_rows, width), center], 0)
    full_weight = lax.all_gather(weight, "gen", axis=0, tiled=True)
    product = jnp.dot(wide, full_weight, preferred_element_type=jnp.float32)
    gen_pre = product[:local_rows].reshape(box_dev, gen_dev, local_cols)
    center_pre = product[local_rows:] + bias
    part_radius = jnp.sum(jnp.abs(gen_pre), axis=1)
    cot_wide = gens_cot.astype(jnp.float32)
    radius = lax.psum(part_radius, "gen")
    slope, center_out, offset = neuron(center_pre, radius, phase)
    gens_out = (slope[:, None, :] * gen_pre).astype(jnp.bfloat16)
    intersection = lax.psum(jnp.sum(cot_wide * gen_pre, axis=1), "gen")
    unused, pull = jax.vjp(lambda a, b: neuron(a, b, phase), center_pre, radius)
    g_center, g_radius = pull((intersection, center_cot, offset_cot))
    gen_back = (slope[:, None, :] * cot_wide + jnp.sign(gen_pre) * g_radius[:, None, :]).astype(
        jnp.bfloat16
    )
    center_back = g_center.astype(jnp.bfloat16)
    back = jnp.concatenate([gen_back.reshape(local_rows, local_cols), center_back], 0)
    first_gen = (lax.axis_index("gen") == 0).astype(jnp.bfloat16)
    back_owned = jnp.concatenate(
        [gen_back.reshape(local_rows, local_cols), center_back * first_gen], 0
    )
    bias_part = jnp.sum(g_center, axis=0)
    shares = lax.psum_scatter(
        lax.dot_general(
            wide, back_owned, (((0,), (0,)), ((), ())), preferred_element_type=jnp.float32
        ),
        "gen",
        scatter_dimension=0,
        tiled=True,
    )
    weight_grad, bias_grad = lax.psum((shares, bias_part), "box")
    partial_back = lax.dot_general(
        back, full_weight, (((1,), (1,)), ((), ())), preferred_element_type=jnp.float32
    )
    summed = lax.psum_scatter(partial_back, "neur", scatter_dimension=1, tiled=True)
    gens_grad = summed[:local_rows].reshape(box_dev, gen_dev, summed.shape[1])
    center_grad = summed[local_rows:]
    return (center_out, gens_out, offset, weight_grad, bias_grad, gens_grad, center_grad)


def solution(mesh):
    return jax.shard_map(
        body,
        mesh=mesh,
        in_specs=(
            P("box", "gen", None),
            P("box", None),
            P("gen", "neur"),
            P("neur"),
            P("box", "neur"),
            P("box", "gen", "neur"),
            P("box", "neur"),
            P("box", "neur"),
        ),
        out_specs=(
            P("box", "neur"),
            P("box", "gen", "neur"),
            P("box", "neur"),
            P("gen", "neur"),
            P("neur"),
            P("box", "gen", "neur"),
            P("box", "neur"),
        ),
        check_vma=False,
    )
```

profile of v0, /device:TPU:1, one launch (start us, length us, event | category | flops | bytes accessed | tf_op | source)
XLA Modules:
  0.0 407.0 jit_solution(1934625204832896701)
XLA Ops:
  7.2 0.0 all-gather.2.cloned.1.call-start
  7.2 0.7 all-gather.2.cloned.1.call-update
  7.9 0.0 reduce-scatter.3.cloned.1.call-start
  8.0 72.6 %all-gather.2.cloned.1.call-done = bf16[4096,512]{1,0:T(8,128)(2,1)} async-done(((bf16[128,512]{1,0:T(8,128)(2,1)}), bf16[4096,512]{1,0:T(8,128)(2,1)}) %all-gather.2.cloned.1.call-update) | async-done | bytes 4194320 | tf_op jit(solution)/shard_map/all_gather | solution.py:23
  80.6 0.0 copy-start.1
  80.6 0.0 copy-start.3
  80.6 0.0 copy-start.4
  80.6 0.0 copy-start.5
  80.6 0.0 copy-start.6
  80.6 0.0 copy-start
  80.6 0.0 copy-start.2
  80.6 3.4 fusion.1
  84.0 0.0 copy-done.1
  84.0 0.1 fusion.4
  84.1 101.8 %all-reduce = (f32[4,512]{1,0:T(4,128)S(1)}, f32[4,512]{1,0:T(4,128)S(1)}) all-reduce(f32[4,512]{1,0:T(4,128)S(1)} %get-tuple-element.8, f32[4,512]{1,0:T(4,128)S(1)} %get-tuple-element.7), channel_id=1, replica_groups=mesh['gen'=32,'neur'=4,'box'=2] {'gen'}, use_global_device_ids=true, to_apply=%region_1.0 | all-reduce | flops 4096 | bytes 32768 | tf_op jit(solution)/shard_map/psum | solution.py:29
  185.9 0.0 copy-done.3
  185.9 0.0 copy-done.4
  185.9 0.0 copy-done.5
  185.9 0.0 copy-done.6
  186.0 0.8 fusion.3
  186.8 0.0 copy-done
  186.8 0.0 copy-done.2
  186.8 4.6 %fusion = f32[4096,512]{1,0:T(8,128)} fusion(bf16[4,4096]{1,0:T(4,128)(2,1)S(1)} %copy-done.2, bf16[128,4096]{1,0:T(8,128)(2,1)S(1)} %bitcast.13, bf16[4,512]{1,0:T(4,128)(2,1)S(1)} %get-tuple-element.16, bf16[128,512]{1,0:T(8,128)(2,1)S(1)} %bitcast.10), kind=kOutput, calls=%fused_computation.1 | convolution fusion | flops 556081152 | bytes 9605120 | tf_op jit(solution)/shard_map/dot_general | solution.py:46
  191.3 0.0 reduce-scatter.3.cloned.1.call-update
  191.4 0.0 reduce-scatter.5.cloned.1.call-start
  191.4 5.1 %fusion.7 = f32[132,4096]{1,0:T(8,128)} fusion(bf16[4096,512]{1,0:T(8,128)(2,1)} %all-gather.2.cloned.1.call-done, bf16[4,512]{1,0:T(4,128)(2,1)S(1)} %get-tuple-element.17, bf16[128,512]{1,0:T(8,128)(2,1)S(1)} %bitcast.11), kind=kOutput, calls=%fused_computation.12 | convolution fusion | flops 553918464 | bytes 6492160 | tf_op jit(solution)/shard_map/dot_general | solution.py:54
  196.5 0.0 reduce-scatter.5.cloned.1.call-update
  196.5 0.0 all-reduce.3.cloned.1.call-start
  196.5 126.5 %reduce-scatter.3.cloned.1.call-done = f32[128,512]{1,0:T(8,128)} async-done(((f32[4096,512]{1,0:T(8,128)}), f32[128,512]{1,0:T(8,128)}) %reduce-scatter.3.cloned.1.call-update) | async-done | bytes 262160 | tf_op jit(solution)/shard_map/reduce_scatter | solution.py:45
  323.1 0.0 all-reduce.3.cloned.1.call-update
  323.1 5.9 %psum.31 = f32[512]{0:T(512)} all-reduce(f32[512]{0:T(512)S(1)} %get-tuple-element.11), channel_id=1, replica_groups=mesh['gen'=32,'neur'=4,'box'=2] {'box'}, use_global_device_ids=true, to_apply=%region_7.8 | all-reduce | flops 512 | bytes 4096 | tf_op jit(solution)/shard_map/psum | solution.py:53
  328.9 0.6 multiply_add_fusion.1
  329.6 30.9 %reduce-scatter.5.cloned.1.call-done = f32[132,1024]{1,0:T(8,128)} async-done(((f32[132,4096]{1,0:T(8,128)}), f32[132,1024]{1,0:T(8,128)}) %reduce-scatter.5.cloned.1.call-update) | async-done | bytes 540688 | tf_op jit(solution)/shard_map/reduce_scatter | solution.py:57
  360.5 1.4 slice.19
  361.9 1.9 slice.18
  363.7 35.1 %all-reduce.3.cloned.1.call-done = f32[128,512]{1,0:T(8,128)} async-done(((f32[128,512]{1,0:T(8,128)}), f32[128,512]{1,0:T(8,128)}) %all-reduce.3.cloned.1.call-update) | async-done | bytes 262160 | tf_op jit(solution)/shard_map/psum | solution.py:53
  398.8 1.7 copy.16
  (4 shorter events, 0.1 us)
Async XLA Ops:
  7.2 73.4 %all-gather.2.cloned.1.call-start = ((), (), s32[]{:S(2)}) async-start(), calls=%async_computation.2 | async-start | bytes 4325376 | tf_op jit(solution)/shard_map/all_gather | solution.py:23
  7.9 315.1 %reduce-scatter.3.cloned.1.call-start = ((), (), s32[]{:S(2)}) async-start(), calls=%async_computation.3 | async-start | bytes 8650752 | tf_op jit(solution)/shard_map/reduce_scatter | solution.py:45
  80.6 3.4 copy-start.1
  80.6 105.3 %copy-start.3 = (f32[4,512]{1,0:T(4,128)S(1)}, f32[4,512]{1,0:T(4,128)}, u32[]{:S(2)}) copy-start(f32[4,512]{1,0:T(4,128)} %param.14) | copy-start | bytes 24580
  80.6 105.3 %copy-start.4 = (f32[4,512]{1,0:T(4,128)S(1)}, f32[4,512]{1,0:T(4,128)}, u32[]{:S(2)}) copy-start(f32[4,512]{1,0:T(4,128)} %param.15) | copy-start | bytes 24580
  80.6 105.3 %copy-start.5 = (s32[4,512]{1,0:T(4,128)S(1)}, s32[4,512]{1,0:T(4,128)}, u32[]{:S(2)}) copy-start(s32[4,512]{1,0:T(4,128)} %param.12) | copy-start | bytes 24580
  80.6 105.3 %copy-start.6 = (f32[512]{0:T(512)S(1)}, f32[512]{0:T(512)}, u32[]{:S(2)}) copy-start(f32[512]{0:T(512)} %param.11) | copy-start | bytes 6148
  80.6 106.2 %copy-start = (bf16[4,32,4096]{2,1,0:T(8,128)(2,1)S(1)}, bf16[4,32,4096]{2,1,0:T(8,128)(2,1)}, u32[]{:S(2)}) copy-start(bf16[4,32,4096]{2,1,0:T(8,128)(2,1)} %param.8) | copy-start | bytes 3145732
  80.6 106.2 %copy-start.2 = (bf16[4,4096]{1,0:T(4,128)(2,1)S(1)}, bf16[4,4096]{1,0:T(4,128)(2,1)}, u32[]{:S(2)}) copy-start(bf16[4,4096]{1,0:T(4,128)(2,1)} %param.9) | copy-start | bytes 98308
  191.4 169.1 %reduce-scatter.5.cloned.1.call-start = ((), (), s32[]{:S(2)}) async-start(), calls=%async_computation.5 | async-start | bytes 2785280 | tf_op jit(solution)/shard_map/reduce_scatter | solution.py:57
  196.5 202.3 %all-reduce.3.cloned.1.call-start = ((), (), s32[]{:S(2)}) async-start(), calls=%async_computation.4 | async-start | bytes 524288 | tf_op jit(solution)/shard_map/psum | solution.py:53
Sparse Core Ops, SparseCore 0:
  9.8 70.6 all-gather.1
  191.5 131.5 reduce-scatter.2
  325.6 34.8 reduce-scatter.4
  362.9 35.8 all-reduce.2
where the time goes:
time: 407 us
  waiting for transfers between devices  266 us (65%)
  blocking collectives  108 us (27%)
  between operations  13.9 us (3%)
  matrix products  13 us (3%)
  local copies, waits for them, and re-layouts  4.95 us (1%)
    reduce_scatter x1, waiting for transfers between devices, body(): lax.psum_scatter(lax.dot_general(wide, back_owned, (((0,), (0,)), ((), ()...  127 us
    psum x1, blocking collectives, body(): radius = lax.psum(part_radius, 'gen')  102 us
    all_gather x1, waiting for transfers between devices, body(): full_weight = lax.all_gather(weight, 'gen', axis=0, tiled=True)  72.6 us
    psum x1, waiting for transfers between devices, body(): weight_grad, bias_grad = lax.psum((shares, bias_part), 'box')  35.1 us
    reduce_scatter x1, waiting for transfers between devices, body(): lax.psum_scatter(partial_back, 'neur', scatter_dimension=1, tiled=True)  30.9 us
  transfers between devices with their start and end apart: 4, of which 4 were waited for; matrix products, arithmetic and copies ran while one was open for 2% of the time, Pallas kernels for 0%

commit v1 on v0

--- a/solution.py
+++ b/solution.py
@@ -26,7 +26,7 @@
     center_pre = product[local_rows:] + bias
     part_radius = jnp.sum(jnp.abs(gen_pre), axis=1)
     cot_wide = gens_cot.astype(jnp.float32)
-    radius = lax.psum(part_radius, "gen")
+    radius = jnp.sum(lax.all_gather(part_radius, axis_name="gen"), axis=0)
     slope, center_out, offset = neuron(center_pre, radius, phase)
     gens_out = (slope[:, None, :] * gen_pre).astype(jnp.bfloat16)
     intersection = lax.psum(jnp.sum(cot_wide * gen_pre, axis=1), "gen")

time: 407 us -> 389 us (0.956)
  blocking collectives: 108 us -> 92.8 us
    psum x1, blocking collectives: 102 us -> 53.7 us  [body(): intersection = lax.psum(jnp.sum(cot_wide * gen_pre, axis=1), 'gen')]
    all_gather x0 -> x1, blocking collectives: none -> 33.2 us  [body(): radius = jnp.sum(lax.all_gather(part_radius, axis_name='gen'), axis=0)]
where the time goes in v1:
time: 389 us; the launch traced here: 388 us
  waiting for transfers between devices  262 us (67%)
  blocking collectives  92.8 us (24%)
  between operations  13.9 us (4%)
  matrix products  12.9 us (3%)
  local copies, waits for them, and re-layouts  4.95 us (1%)
    reduce_scatter x1, waiting for transfers between devices, body(): lax.psum_scatter(lax.dot_general(wide, back_owned, (((0,), (0,)), ((), ()...  123 us
    all_gather x1, waiting for transfers between devices, body(): full_weight = lax.all_gather(weight, 'gen', axis=0, tiled=True)  72.6 us
    psum x1, blocking collectives, body(): intersection = lax.psum(jnp.sum(cot_wide * gen_pre, axis=1), 'gen')  53.7 us
    psum x1, waiting for transfers between devices, body(): weight_grad, bias_grad = lax.psum((shares, bias_part), 'box')  35 us
    all_gather x1, blocking collectives, body(): radius = jnp.sum(lax.all_gather(part_radius, axis_name='gen'), axis=0)  33.2 us
    reduce_scatter x1, waiting for transfers between devices, body(): lax.psum_scatter(partial_back, 'neur', scatter_dimension=1, tiled=True)  31.2 us
  transfers between devices with their start and end apart: 4, of which 4 were waited for; matrix products, arithmetic and copies ran while one was open for 2% of the time, Pallas kernels for 0%

profile of v1, /device:TPU:1, one launch (start us, length us, event | category | flops | bytes accessed | tf_op | source)
XLA Modules:
  0.0 388.5 jit_solution(7551191972071794625)
XLA Ops:
  7.2 0.0 all-gather.4.cloned.1.call-start
  7.2 0.7 all-gather.4.cloned.1.call-update
  7.9 0.0 reduce-scatter.3.cloned.1.call-start
  8.0 72.6 %all-gather.4.cloned.1.call-done = bf16[4096,512]{1,0:T(8,128)(2,1)} async-done(((bf16[128,512]{1,0:T(8,128)(2,1)}), bf16[4096,512]{1,0:T(8,128)(2,1)}) %all-gather.4.cloned.1.call-update) | async-done | bytes 4194320 | tf_op jit(solution)/shard_map/all_gather | solution.py:23
  80.6 0.0 copy-start.1
  80.6 0.0 copy-start.3
  80.6 0.0 copy-start.4
  80.6 0.0 copy-start.5
  80.6 0.0 copy-start.6
  80.6 0.0 copy-start.2
  80.6 3.3 fusion.1
  83.9 0.0 copy-done.1
  83.9 0.0 copy-start
  83.9 0.1 fusion.4
  84.0 53.7 %psum.21 = f32[4,512]{1,0:T(4,128)S(1)} all-reduce(f32[4,512]{1,0:T(4,128)S(1)} %get-tuple-element.7), channel_id=1, replica_groups=mesh['gen'=32,'neur'=4,'box'=2] {'gen'}, use_global_device_ids=true, to_apply=%region_3.4 | all-reduce | flops 2048 | bytes 16384 | tf_op jit(solution)/shard_map/psum | solution.py:32
  137.8 33.2 %all-gather.1 = f32[32,4,512]{2,1,0:T(4,128)S(1)} all-gather(f32[1,4,512]{2,1,0:T(4,128)S(1)} %bitcast.16), channel_id=2, replica_groups=mesh['gen'=32,'neur'=4,'box'=2] {'gen'}, dimensions={0}, use_global_device_ids=true | all-gather | bytes 270336 | tf_op jit(solution)/shard_map/all_gather | solution.py:29
  171.0 0.1 reduce_sum.37
  171.0 0.0 copy-done.3
  171.0 0.0 copy-done.4
  171.0 0.0 copy-done.5
  171.0 0.0 copy-done.6
  171.2 0.8 fusion.3
  171.9 0.0 copy-done.2
  171.9 0.0 copy-done
  171.9 4.6 %fusion = f32[4096,512]{1,0:T(8,128)} fusion(bf16[4,4096]{1,0:T(4,128)(2,1)S(1)} %copy-done.2, bf16[128,4096]{1,0:T(8,128)(2,1)S(1)} %bitcast.14, bf16[4,512]{1,0:T(4,128)(2,1)S(1)} %get-tuple-element.14, bf16[128,512]{1,0:T(8,128)(2,1)S(1)} %bitcast.11), kind=kOutput, calls=%fused_computation.1 | convolution fusion | flops 556081152 | bytes 9605120 | tf_op jit(solution)/shard_map/dot_general | solution.py:46
  176.5 0.0 reduce-scatter.3.cloned.1.call-update
  176.5 0.0 reduce-scatter.5.cloned.1.call-start
  176.6 5.1 %fusion.7 = f32[132,4096]{1,0:T(8,128)} fusion(bf16[4096,512]{1,0:T(8,128)(2,1)} %all-gather.4.cloned.1.call-done, bf16[4,512]{1,0:T(4,128)(2,1)S(1)} %get-tuple-element.15, bf16[128,512]{1,0:T(8,128)(2,1)S(1)} %bitcast.12), kind=kOutput, calls=%fused_computation.12 | convolution fusion | flops 553918464 | bytes 6492160 | tf_op jit(solution)/shard_map/dot_general | solution.py:54
  181.6 0.0 reduce-scatter.5.cloned.1.call-update
  181.7 0.0 all-reduce.2.cloned.1.call-start
  181.7 122.5 %reduce-scatter.3.cloned.1.call-done = f32[128,512]{1,0:T(8,128)} async-done(((f32[4096,512]{1,0:T(8,128)}), f32[128,512]{1,0:T(8,128)}) %reduce-scatter.3.cloned.1.call-update) | async-done | bytes 262160 | tf_op jit(solution)/shard_map/reduce_scatter | solution.py:45
  304.2 0.0 all-reduce.2.cloned.1.call-update
  304.3 5.9 %psum.23 = f32[512]{0:T(512)} all-reduce(f32[512]{0:T(512)S(1)} %get-tuple-element.9), channel_id=1, replica_groups=mesh['gen'=32,'neur'=4,'box'=2] {'box'}, use_global_device_ids=true, to_apply=%region_7.8 | all-reduce | flops 512 | bytes 4096 | tf_op jit(solution)/shard_map/psum | solution.py:53
  310.1 0.6 multiply_add_fusion.1
  310.7 31.2 %reduce-scatter.5.cloned.1.call-done = f32[132,1024]{1,0:T(8,128)} async-done(((f32[132,4096]{1,0:T(8,128)}), f32[132,1024]{1,0:T(8,128)}) %reduce-scatter.5.cloned.1.call-update) | async-done | bytes 540688 | tf_op jit(solution)/shard_map/reduce_scatter | solution.py:57
  342.0 1.4 slice.19
  343.3 1.9 slice.18
  345.2 35.0 %all-reduce.2.cloned.1.call-done = f32[128,512]{1,0:T(8,128)} async-done(((f32[128,512]{1,0:T(8,128)}), f32[128,512]{1,0:T(8,128)}) %all-reduce.2.cloned.1.call-update) | async-done | bytes 262160 | tf_op jit(solution)/shard_map/psum | solution.py:53
  380.3 1.7 copy.16
  (4 shorter events, 0.1 us)
Async XLA Ops:
  7.2 73.4 %all-gather.4.cloned.1.call-start = ((), (), s32[]{:S(2)}) async-start(), calls=%async_computation.2 | async-start | bytes 4325376 | tf_op jit(solution)/shard_map/all_gather | solution.py:23
  7.9 296.3 %reduce-scatter.3.cloned.1.call-start = ((), (), s32[]{:S(2)}) async-start(), calls=%async_computation.3 | async-start | bytes 8650752 | tf_op jit(solution)/shard_map/reduce_scatter | solution.py:45
  80.6 3.3 copy-start.1
  80.6 90.5 %copy-start.3 = (f32[4,512]{1,0:T(4,128)S(1)}, f32[4,512]{1,0:T(4,128)}, u32[]{:S(2)}) copy-start(f32[4,512]{1,0:T(4,128)} %param.14) | copy-start | bytes 24580
  80.6 90.5 %copy-start.4 = (f32[4,512]{1,0:T(4,128)S(1)}, f32[4,512]{1,0:T(4,128)}, u32[]{:S(2)}) copy-start(f32[4,512]{1,0:T(4,128)} %param.15) | copy-start | bytes 24580
  80.6 90.5 %copy-start.5 = (s32[4,512]{1,0:T(4,128)S(1)}, s32[4,512]{1,0:T(4,128)}, u32[]{:S(2)}) copy-start(s32[4,512]{1,0:T(4,128)} %param.12) | copy-start | bytes 24580
  80.6 90.5 %copy-start.6 = (f32[512]{0:T(512)S(1)}, f32[512]{0:T(512)}, u32[]{:S(2)}) copy-start(f32[512]{0:T(512)} %param.11) | copy-start | bytes 6148
  80.6 91.4 %copy-start.2 = (bf16[4,4096]{1,0:T(4,128)(2,1)S(1)}, bf16[4,4096]{1,0:T(4,128)(2,1)}, u32[]{:S(2)}) copy-start(bf16[4,4096]{1,0:T(4,128)(2,1)} %param.9) | copy-start | bytes 98308
  83.9 88.0 %copy-start = (bf16[4,32,4096]{2,1,0:T(8,128)(2,1)S(1)}, bf16[4,32,4096]{2,1,0:T(8,128)(2,1)}, u32[]{:S(2)}) copy-start(bf16[4,32,4096]{2,1,0:T(8,128)(2,1)} %param.8) | copy-start | bytes 3145732
  176.5 165.4 %reduce-scatter.5.cloned.1.call-start = ((), (), s32[]{:S(2)}) async-start(), calls=%async_computation.5 | async-start | bytes 2785280 | tf_op jit(solution)/shard_map/reduce_scatter | solution.py:57
  181.7 198.6 %all-reduce.2.cloned.1.call-start = ((), (), s32[]{:S(2)}) async-start(), calls=%async_computation.4 | async-start | bytes 524288 | tf_op jit(solution)/shard_map/psum | solution.py:53
Sparse Core Ops, SparseCore 0:
  9.8 70.6 all-gather.3
  176.6 127.5 reduce-scatter.2
  306.8 35.0 reduce-scatter.4
  344.4 35.8 all-reduce.1
